TPU v7x, 32 devices: a whole 2x2x4 slice. The times are simulated.
32 devices in a mesh: team: 8 (over z, core), member: 4 (over y, x).
Axes of the slice: x: 2, y: 2, z: 4, core: 2. Of those that a mesh axis runs over, the one named last changes fastest.
Arguments:
- state_start: float32 [24, 512, 512], P(None, 'team', 'member'), may hold values from -6 to 6
- state_section: float32 [24, 512, 512], P(None, 'team', 'member'), may hold values from -6 to 6
- velocity: float32 [2, 512, 512], P(None, 'team', 'member'), may hold values from -3 to 3
- diffusivity: float32 [24], replicated, may hold values from 0.05 to 0.5
- flame_cells: int32 [32, 128], P(('team', 'member')), may hold values from 0 to 8191, as said below
- block_team: int32 [32, 1], replicated, may hold values from 0 to 7; in each aligned block of 4 rows (0 to 3, 4 to 7, ...) at most 2 rows name the same one
- w_in: bfloat16 [8, 4, 1600, 24], P('team', 'member'), may hold values from -1.25 to 1.25
- w_mid: bfloat16 [8, 4, 800, 1600], P('team', 'member'), may hold values from -0.15625 to 0.15625
- w_low: bfloat16 [8, 4, 400, 800], P('team', 'member'), may hold values from -0.21875 to 0.21875
- w_out: bfloat16 [8, 4, 24, 400], P('team', 'member'), may hold values from -0.3125 to 0.3125
Outputs:
- source_rates: float32 [24, 512, 512], P(None, 'team', 'member')
- new_state: float32 [24, 512, 512], P(None, 'team', 'member')
Inputs may be any that keep to these rules, and one draw needn't show every extreme that they name: `flame_cells`: the 128 entries of the rows of one device (rows d * 1 to d + 1 - 1) are distinct cells of that device's tile, given as i * 128 + j. `block_team`: in each aligned block of 4 rows (the flame blocks of one index of team) no regime appears more than 2 times.
All inputs are finite; a program needn't handle non-finite values.
Results may differ from a plain program's by a relative error of at most 0.0017.
The roundings to bfloat16 on the way count: a program that leaves them out, or rounds other values in their place, can miss the bound.
Values may be sent and summed in bfloat16 or wider, within the bound.
A program may use at most 64 MiB of HBM per device.

v0:
```python
import math
import jax
import jax.numpy as jnp
from jax import lax
from jax.sharding import PartitionSpec as P

BLK_DEV = 1
CAP = 2
TIME_STEP = 0.25


def padded_2(block, sides, width):
    for axis, dim in sides:
        count = lax.axis_size(axis)
        forward = [(i, i + 1) for i in range(count - 1)]
        forward.append((count - 1, 0))
        backward = [(target, source) for source, target in forward]
        low = lax.ppermute(
            lax.slice_in_dim(block, block.shape[dim] - width, None, axis=dim), axis, forward
        )
        high = lax.ppermute(lax.slice_in_dim(block, 0, width, axis=dim), axis, backward)
        block = jnp.concatenate([low, block, high], axis=dim)
    return block


def build_slots(assigned, regimes, capacity):
    regime_ids = jnp.arange(regimes, dtype=jnp.int32)
    onehot = (assigned[:, None] == regime_ids[None, :]).astype(jnp.int32)
    ranks = jnp.sum((jnp.cumsum(onehot, axis=0) - onehot) * onehot, axis=1)
    slot_ids = jnp.arange(capacity, dtype=jnp.int32)
    row_ids = jnp.arange(assigned.shape[0], dtype=jnp.int32)
    match_regime = assigned[None, None, :] == regime_ids[:, None, None]
    match_rank = ranks[None, None, :] == slot_ids[None, :, None]
    matched = (match_regime & match_rank).astype(jnp.int32)
    slot_row = jnp.sum(matched * row_ids[None, None, :], axis=2)
    slot_valid = jnp.sum(matched, axis=2) > 0
    return (ranks, slot_row, slot_valid)


def shards(
    state_start,
    state_section,
    velocity,
    diffusivity,
    flame_cells,
    block_team,
    w_in,
    w_mid,
    w_low,
    w_out,
):
    regimes = lax.axis_size("team")
    members = lax.axis_size("member")
    fields, rows_x, rows_y = state_section.shape
    block_cells = flame_cells.shape[1]
    row_blocks = members * BLK_DEV
    slot_width = CAP * block_cells
    team_index = lax.axis_index("team")
    padded = padded_2(state_section.astype(jnp.bfloat16), (("team", 1), ("member", 2)), 1).astype(
        state_section.dtype
    )
    plus_x = padded[:, 2:, 1:-1]
    minus_x = padded[:, :-2, 1:-1]
    plus_y = padded[:, 1:-1, 2:]
    minus_y = padded[:, 1:-1, :-2]
    spread = diffusivity[:, None, None] * (
        plus_x + minus_x + plus_y + minus_y - 4.0 * state_section
    )
    advect = 0.5 * velocity[0][None] * (plus_x - minus_x) + 0.5 * velocity[1][None] * (
        plus_y - minus_y
    )
    flow = spread - advect
    assigned = lax.dynamic_slice_in_dim(block_team[:, 0], team_index * row_blocks, row_blocks)
    ranks, slot_row, slot_valid = build_slots(assigned, regimes, CAP)
    flat_section = state_section.reshape(fields, rows_x * rows_y)
    own_states = jnp.transpose(jnp.take(flat_section, flame_cells, axis=1), (1, 0, 2)).astype(
        jnp.bfloat16
    )
    row_states = lax.all_gather(own_states, "member", axis=0, tiled=True)
    picked = jnp.take(row_states, slot_row.reshape(-1), axis=0).reshape(
        regimes, CAP, fields, block_cells
    )
    picked = jnp.where(slot_valid[:, :, None, None], picked, jnp.zeros_like(picked))
    outgoing = jnp.transpose(picked, (0, 2, 1, 3)).reshape(regimes, fields, slot_width)
    incoming = lax.all_to_all(outgoing, "team", split_axis=0, concat_axis=0, tiled=True)
    weight_in = w_in[0, 0]
    weight_mid = w_mid[0, 0]
    weight_low = w_low[0, 0]
    weight_out = w_out[0, 0]
    group_size = math.gcd(regimes, max(1, 1024 // slot_width))
    grouped = incoming.reshape(regimes // group_size, group_size, fields, slot_width)

    def run_group(states):
        layer_one = jnp.einsum("hf,gfk->hgk", weight_in, states, preferred_element_type=jnp.float32)
        hidden_one = jax.nn.silu(layer_one).astype(jnp.bfloat16)
        layer_two = jnp.einsum(
            "ih,hgk->igk", weight_mid, hidden_one, preferred_element_type=jnp.float32
        )
        hidden_two = jax.nn.silu(layer_two).astype(jnp.bfloat16)
        layer_three = jnp.einsum(
            "ji,igk->jgk", weight_low, hidden_two, preferred_element_type=jnp.float32
        )
        hidden_three = jax.nn.silu(layer_three).astype(jnp.bfloat16)
        return jnp.einsum(
            "fj,jgk->gfk", weight_out, hidden_three, preferred_element_type=jnp.float32
        )

    produced = lax.map(run_group, grouped).reshape(regimes, fields, slot_width)
    returned = lax.all_to_all(produced, "team", split_axis=0, concat_axis=0, tiled=True)
    slot_rates = returned.reshape(regimes, fields, CAP, block_cells)
    row_terms = slot_rates[assigned, :, ranks]
    own_rates = lax.psum_scatter(row_terms, "member", scatter_dimension=0, tiled=True)
    flat_rates = jnp.zeros((fields, rows_x * rows_y), jnp.float32)
    flat_rates = flat_rates.at[:, flame_cells].add(jnp.transpose(own_rates, (1, 0, 2)))
    source_rates = flat_rates.reshape(fields, rows_x, rows_y)
    new_state = 0.75 * state_start + 0.25 * (state_section + TIME_STEP * (flow + source_rates))
    return (source_rates, new_state)


def solution(mesh):
    placed = (
        P(None, "team", "member"),
        P(None, "team", "member"),
        P(None, "team", "member"),
        P(),
        P(("team", "member"), None),
        P(),
        P("team", "member", None, None),
        P("team", "member", None, None),
        P("team", "member", None, None),
        P("team", "member", None, None),
    )
    return jax.shard_map(
        shards,
        mesh=mesh,
        in_specs=placed,
        out_specs=(P(None, "team", "member"), P(None, "team", "member")),
        check_vma=False,
    )
```

profile of v0, /device:TPU:0, one launch (start us, length us, event | category | flops | bytes accessed | tf_op | source)
XLA Modules:
  0.0 117.3 jit_solution(2329103246357906596)
XLA Ops:
  7.2 0.8 fusion.50
  8.2 0.7 fusion.51
  8.9 0.7 and_bitcast_fusion
  9.6 0.2 select_reduce_fusion
  10.3 2.8 %copy.52 = bf16[24,64,128]{0,2,1:T(8,128)(2,1)} copy(f32[24,64,128]{2,1,0:T(8,128)} %param.13) | data formatting | bytes 1179648 | tf_op args[1]
  13.0 2.5 %gather_fusion = bf16[128,24]{1,0:T(8,128)(2,1)S(1)} fusion(bf16[24,8192]{0,1:T(8,128)(2,1)} %bitcast.134, s32[1024]{0:T(1024)S(1)} %pad_clamp_fusion.1), kind=kCustom, calls=%fused_computation | custom fusion | bytes 12800 | tf_op jit(solution)/shard_map/jit(_take)/gather | solution.py:76
  15.7 9.7 %all_gather.3 = bf16[4,24,128]{2,1,0:T(8,128)(2,1)S(1)} all-gather(bf16[1,24,128]{2,1,0:T(8,128)(2,1)S(1)} %fusion.39), channel_id=1, replica_groups=mesh['team'=8,'member'=4] {'member'}, dimensions={0}, use_global_device_ids=true | all-gather | bytes 30720 | tf_op jit(solution)/shard_map/all_gather | solution.py:79
  25.3 0.6 gather_fusion.1
  26.1 0.7 reshape.185
  26.8 4.9 %all-to-all-start = ((bf16[8,24,256]{2,1,0:T(8,128)(2,1)}), bf16[8,24,256]{2,1,0:T(8,128)(2,1)S(1)}, u32[]{:S(2)}, u32[]{:S(2)}) async-start(bf16[8,24,256]{2,1,0:T(8,128)(2,1)} %reshape.185), calls=%async_computation | async-start | bytes 196608 | tf_op jit(solution)/shard_map/all_to_all | solution.py:85
  31.8 0.6 collective-permute-start
  32.3 3.1 %collective-permute-start.1 = (bf16[24,1,128]{2,1,0:T(2,128)(2,1)S(1)}, bf16[24,1,128]{2,1,0:T(2,128)(2,1)S(1)}, u32[]{:S(2)}, u32[]{:S(2)}) collective-permute-start(bf16[24,1,128]{2,1,0:T(2,128)(2,1)S(1)} %get-tuple-element.73), channel_id=1, source_target_pairs={{4,0},{8,4},{12,8},{16,12},{20,16},{24,20},{28,24},{0,28},{5,1},{9... | collective-permute-start | bytes 18440 | tf_op jit(solution)/shard_map/ppermute | solution.py:21
  35.5 2.6 %all-to-all-done = bf16[8,24,256]{2,1,0:T(8,128)(2,1)S(1)} async-done(((bf16[8,24,256]{2,1,0:T(8,128)(2,1)}), bf16[8,24,256]{2,1,0:T(8,128)(2,1)S(1)}, u32[]{:S(2)}, u32[]{:S(2)}) %all-to-all-start) | async-done | bytes 98336 | tf_op jit(solution)/shard_map/all_to_all | solution.py:85
  38.1 24.8 %while.10 = (s32[]{:T(128)}, f32[2,4,24,256]{3,2,1,0:T(8,128)}, bf16[2,4,24,256]{3,2,1,0:T(8,128)(2,1)S(1)}, bf16[1600,24]{0,1:T(8,128)(2,1)S(1)}, bf16[800,1600...) while((s32[]{:T(128)}, f32[2,4,24,256]{3,2,1,0:T(8,128)}, ...), condition=%wide.region_5.6_spmd, body=%wide.region_4.5_spmd.sunk | while | flops 3389440000 | bytes 10000729 | solution.py:108
  38.1 7.9 %fusion.71 = f32[4,256,800]{1,2,0:T(8,128)} fusion(bf16[800,1600]{1,0:T(8,128)(2,1)} %get-tuple-element.141, bf16[1600,24]{0,1:T(8,128)(2,1)S(1)} %get-tuple-element.140, bf16[2,4,24,256]{3,2,1,0:T(8,128)(2,1)S(1)} %get-tuple-element.139, s32[]{:T(128)} %get-tuple-element.129), kind=kOutput, calls=%fused_computation.16.clone.1 | convolution fusion | flops 2708275200 | bytes 5965828 | tf_op jit(solution)/shard_map/while/body/eval_jaxpr/ih,hgk->igk/dot_general | solution.py:96
  46.1 4.5 %fusion.72 = f32[2,4,24,256]{3,2,1,0:T(8,128)} fusion(f32[2,4,24,256]{3,2,1,0:T(8,128)} %get-tuple-element.130, s32[]{:T(128)} %get-tuple-element.129, f32[4,256,800]{1,2,0:T(8,128)} %fusion.71, bf16[400,800]{1,0:T(8,128)(2,1)S(1)} %get-tuple-element.142, bf16[24,400]{1,0:T(8,128)(2,1)S(1)} %get-tuple-element.143), kind=kOutput, calls=%fused_computation.26.clone.1 | convolution fusion | flops 681164800 | bytes 4034816 | tf_op jit(solution)/shard_map/while/body/eval_jaxpr/fj,jgk->gfk/dot_general | solution.py:104
  50.5 7.9 %fusion.71 = f32[4,256,800]{1,2,0:T(8,128)} fusion(bf16[800,1600]{1,0:T(8,128)(2,1)} %get-tuple-element.141, bf16[1600,24]{0,1:T(8,128)(2,1)S(1)} %get-tuple-element.140, bf16[2,4,24,256]{3,2,1,0:T(8,128)(2,1)S(1)} %get-tuple-element.139, s32[]{:T(128)} %get-tuple-element.129), kind=kOutput, calls=%fused_computation.16.clone.1 | convolution fusion | flops 2708275200 | bytes 5965828 | tf_op jit(solution)/shard_map/while/body/eval_jaxpr/ih,hgk->igk/dot_general | solution.py:96
  58.4 4.4 %fusion.72 = f32[2,4,24,256]{3,2,1,0:T(8,128)} fusion(f32[2,4,24,256]{3,2,1,0:T(8,128)} %get-tuple-element.130, s32[]{:T(128)} %get-tuple-element.129, f32[4,256,800]{1,2,0:T(8,128)} %fusion.71, bf16[400,800]{1,0:T(8,128)(2,1)S(1)} %get-tuple-element.142, bf16[24,400]{1,0:T(8,128)(2,1)S(1)} %get-tuple-element.143), kind=kOutput, calls=%fused_computation.26.clone.1 | convolution fusion | flops 681164800 | bytes 4034816 | tf_op jit(solution)/shard_map/while/body/eval_jaxpr/fj,jgk->gfk/dot_general | solution.py:104
  62.9 3.4 %all-to-all-start.1 = ((f32[8,24,256]{2,1,0:T(8,128)}), f32[8,24,256]{2,1,0:T(8,128)S(1)}, u32[]{:S(2)}, u32[]{:S(2)}) async-start(f32[8,24,256]{2,1,0:T(8,128)} %bitcast.24), calls=%async_computation.1 | async-start | bytes 393216 | tf_op jit(solution)/shard_map/all_to_all | solution.py:109
  66.5 0.2 fusion.52
  66.7 1.5 %collective-permute-start.2 = (bf16[24,66,1]{2,1,0:T(8,128)(2,1)S(1)}, bf16[24,66,1]{2,1,0:T(8,128)(2,1)S(1)}, u32[]{:S(2)}, u32[]{:S(2)}) collective-permute-start(bf16[24,66,1]{2,1,0:T(8,128)(2,1)S(1)} %get-tuple-element.70), channel_id=1, source_target_pairs={{0,1},{1,2},{2,3},{3,0},{4,5},{5,6},{6,7},{7,4},{8,9},{9,10},{10,1... | collective-permute-start | bytes 9512 | tf_op jit(solution)/shard_map/ppermute | solution.py:18
  68.3 1.4 %collective-permute-start.3 = (bf16[24,66,1]{2,1,0:T(8,128)(2,1)S(1)}, bf16[24,66,1]{2,1,0:T(8,128)(2,1)}, u32[]{:S(2)}, u32[]{:S(2)}) collective-permute-start(bf16[24,66,1]{2,1,0:T(8,128)(2,1)S(1)} %get-tuple-element.71), channel_id=1, source_target_pairs={{1,0},{2,1},{3,2},{0,3},{5,4},{6,5},{7,6},{4,7},{9,8},{10,9},{11,1... | collective-permute-start | bytes 9512 | tf_op jit(solution)/shard_map/ppermute | solution.py:21
  69.7 4.8 %all-to-all-done.1 = f32[8,24,256]{2,1,0:T(8,128)S(1)} async-done(((f32[8,24,256]{2,1,0:T(8,128)}), f32[8,24,256]{2,1,0:T(8,128)S(1)}, u32[]{:S(2)}, u32[]{:S(2)}) %all-to-all-start.1) | async-done | bytes 196640 | tf_op jit(solution)/shard_map/all_to_all | solution.py:109
  74.5 1.2 %gather_fusion.2 = f32[4,24,128]{2,1,0:T(8,128)} fusion(f32[8,24,2,128]{3,1,2,0:T(8,128)S(1)} %copy_bitcast_fusion, s32[4]{0:T(128)S(1)} %fusion.49), kind=kCustom, calls=%fused_computation.2 | custom fusion | bytes 98336 | tf_op jit(solution)/shard_map/gather | solution.py:111
  75.7 5.0 %collective-permute-done.2 = bf16[24,66,1]{2,1,0:T(8,128)(2,1)S(1)} collective-permute-done((bf16[24,66,1]{2,1,0:T(8,128)(2,1)S(1)}, bf16[24,66,1]{2,1,0:T(8,128)(2,1)S(1)}, u32[]{:S(2)}, u32[]{:S(2)}) %collective-permute-start.2) | collective-permute-done | bytes 3200 | tf_op jit(solution)/shard_map/ppermute | solution.py:18
  80.7 9.3 %collective-permute-done.3 = bf16[24,66,1]{2,1,0:T(8,128)(2,1)} collective-permute-done((bf16[24,66,1]{2,1,0:T(8,128)(2,1)S(1)}, bf16[24,66,1]{2,1,0:T(8,128)(2,1)}, u32[]{:S(2)}, u32[]{:S(2)}) %collective-permute-start.3) | collective-permute-done | bytes 3200 | tf_op jit(solution)/shard_map/ppermute | solution.py:21
  90.0 1.7 %maximum_convert_fusion = f32[24,66,130]{2,1,0:T(8,128)S(1)} fusion(bf16[24,66,1]{2,1,0:T(8,128)(2,1)} %collective-permute-done.3, bf16[24,1,128]{2,1,0:T(2,128)(2,1)S(1)} %collective-permute-done.1, bf16[24,64,128]{2,1,0:T(8,128)(2,1)S(1)} %convert_element_type.35, bf16[24,1,128]{2,1,0:T(2,128)(2,1)S(1)} %collective-permute-done, ...), kind=kLoop, calls=%fused_computation.37 | loop fusion | flops 2059200 | bytes 1235520 | tf_op jit(solution)/shard_map/convert_element_type | solution.py:59
  91.7 8.6 %reduce-scatter.4.cloned.1.call-done = f32[1,24,128]{2,1,0:T(8,128)} async-done(((f32[4,24,128]{2,1,0:T(8,128)}), f32[1,24,128]{2,1,0:T(8,128)}) %reduce-scatter.4.cloned.1.call-update) | async-done | bytes 12304
  100.3 0.8 copy.57
  101.1 3.2 %scatter_custom_fusion = f32[24,8192]{0,1:T(8,128)} fusion(s32[128]{0:T(128)S(1)} %fusion.51, f32[128,24]{1,0:T(8,128)S(1)} %copy.57, f32[]{:T(128)} %constant.35.clone.1), kind=kCustom, calls=%fused_computation.35 | custom fusion | flops 3072 | bytes 786436 | tf_op jit(solution)/shard_map/scatter-add | solution.py:114
  104.3 2.9 %copy.59 = f32[24,64,128]{2,1,0:T(8,128)S(1)} copy(f32[24,64,128]{0,2,1:T(8,128)} %bitcast.133) | data formatting | bytes 1572864
  107.3 3.2 %multiply_add_fusion = f32[24,64,128]{2,1,0:T(8,128)} fusion(f32[24,64,128]{2,1,0:T(8,128)S(1)} %copy-done, f32[24,64,128]{2,1,0:T(8,128)S(1)} %copy.59, f32[24,66,130]{2,1,0:T(8,128)S(1)} %maximum_convert_fusion, f32[24,64,128]{2,1,0:T(8,128)} %param.12, f32[64,128]{1,0:T(8,128)S(1)} %get-tuple-element.75, f32[64,128]{1,0:T(8,128)S(1)} %get-tuple-element.74, ...), kind=kLoop, calls=%fused_computation.38 | loop fusion | flops 3538944 | bytes 6357088 | tf_op jit(solution)/shard_map/add | solution.py:116
  (43 shorter events, 1.4 us)
Async XLA Ops:
  7.2 28.3 %copy-start.4 = (s32[32,1]{0,1:T(1,128)S(1)}, s32[32,1]{0,1:T(1,128)}, u32[]{:S(2)}) copy-start(s32[32,1]{0,1:T(1,128)} %param.17) | copy-start | bytes 388
  7.2 24.5 %copy-start = (f32[24,64,128]{2,1,0:T(8,128)S(1)}, f32[24,64,128]{2,1,0:T(8,128)}, u32[]{:S(2)}) copy-start(f32[24,64,128]{2,1,0:T(8,128)} %param.13) | copy-start | bytes 2359300
  7.2 28.2 %copy-start.2 = (f32[2,64,128]{2,1,0:T(8,128)S(1)}, f32[2,64,128]{2,1,0:T(8,128)}, u32[]{:S(2)}) copy-start(f32[2,64,128]{2,1,0:T(8,128)} %param.14) | copy-start | bytes 196612
  7.2 30.9 %copy-start.6 = (bf16[1,1,1600,24]{2,3,1,0:T(8,128)(2,1)S(1)}, bf16[1,1,1600,24]{2,3,1,0:T(8,128)(2,1)}, u32[]{:S(2)}) copy-start(bf16[1,1,1600,24]{2,3,1,0:T(8,128)(2,1)} %param.18) | copy-start | bytes 230404
  7.2 30.9 %copy-start.5 = (bf16[1,1,400,800]{3,2,1,0:T(8,128)(2,1)S(1)}, bf16[1,1,400,800]{3,2,1,0:T(8,128)(2,1)}, u32[]{:S(2)}) copy-start(bf16[1,1,400,800]{3,2,1,0:T(8,128)(2,1)} %param.20) | copy-start | bytes 1920004
  7.2 30.9 %copy-start.7 = (bf16[1,1,24,400]{3,2,1,0:T(8,128)(2,1)S(1)}, bf16[1,1,24,400]{3,2,1,0:T(8,128)(2,1)}, u32[]{:S(2)}) copy-start(bf16[1,1,24,400]{3,2,1,0:T(8,128)(2,1)} %param.21) | copy-start | bytes 57604
  26.8 11.3 %all-to-all-start = ((bf16[8,24,256]{2,1,0:T(8,128)(2,1)}), bf16[8,24,256]{2,1,0:T(8,128)(2,1)S(1)}, u32[]{:S(2)}, u32[]{:S(2)}) async-start(bf16[8,24,256]{2,1,0:T(8,128)(2,1)} %reshape.185), calls=%async_computation | async-start | bytes 196608 | tf_op jit(solution)/shard_map/all_to_all | solution.py:85
  31.8 34.6 %collective-permute-start = (bf16[24,1,128]{2,1,0:T(2,128)(2,1)S(1)}, bf16[24,1,128]{2,1,0:T(2,128)(2,1)S(1)}, u32[]{:S(2)}, u32[]{:S(2)}) collective-permute-start(bf16[24,1,128]{2,1,0:T(2,128)(2,1)S(1)} %get-tuple-element.72), channel_id=1, source_target_pairs={{0,4},{4,8},{8,12},{12,16},{16,20},{20,24},{24,28},{28,0},{1,5},{5... | collective-permute-start | bytes 18440 | tf_op jit(solution)/shard_map/ppermute | solution.py:18
  32.3 34.0 %collective-permute-start.1 = (bf16[24,1,128]{2,1,0:T(2,128)(2,1)S(1)}, bf16[24,1,128]{2,1,0:T(2,128)(2,1)S(1)}, u32[]{:S(2)}, u32[]{:S(2)}) collective-permute-start(bf16[24,1,128]{2,1,0:T(2,128)(2,1)S(1)} %get-tuple-element.73), channel_id=1, source_target_pairs={{4,0},{8,4},{12,8},{16,12},{20,16},{24,20},{28,24},{0,28},{5,1},{9... | collective-permute-start | bytes 18440 | tf_op jit(solution)/shard_map/ppermute | solution.py:21
  62.9 11.6 %all-to-all-start.1 = ((f32[8,24,256]{2,1,0:T(8,128)}), f32[8,24,256]{2,1,0:T(8,128)S(1)}, u32[]{:S(2)}, u32[]{:S(2)}) async-start(f32[8,24,256]{2,1,0:T(8,128)} %bitcast.24), calls=%async_computation.1 | async-start | bytes 393216 | tf_op jit(solution)/shard_map/all_to_all | solution.py:109
  66.3 34.0 %reduce-scatter.4.cloned.1.call-start = ((), (), s32[]{:S(2)}) async-start(), calls=%async_computation.3 | async-start | bytes 61440
  66.7 14.0 %collective-permute-start.2 = (bf16[24,66,1]{2,1,0:T(8,128)(2,1)S(1)}, bf16[24,66,1]{2,1,0:T(8,128)(2,1)S(1)}, u32[]{:S(2)}, u32[]{:S(2)}) collective-permute-start(bf16[24,66,1]{2,1,0:T(8,128)(2,1)S(1)} %get-tuple-element.70), channel_id=1, source_target_pairs={{0,1},{1,2},{2,3},{3,0},{4,5},{5,6},{6,7},{7,4},{8,9},{9,10},{10,1... | collective-permute-start | bytes 9512 | tf_op jit(solution)/shard_map/ppermute | solution.py:18
  68.3 21.7 %collective-permute-start.3 = (bf16[24,66,1]{2,1,0:T(8,128)(2,1)S(1)}, bf16[24,66,1]{2,1,0:T(8,128)(2,1)}, u32[]{:S(2)}, u32[]{:S(2)}) collective-permute-start(bf16[24,66,1]{2,1,0:T(8,128)(2,1)S(1)} %get-tuple-element.71), channel_id=1, source_target_pairs={{1,0},{2,1},{3,2},{0,3},{5,4},{6,5},{7,6},{4,7},{9,8},{10,9},{11,1... | collective-permute-start | bytes 9512 | tf_op jit(solution)/shard_map/ppermute | solution.py:21
  104.3 3.0 %copy-start.3 = (f32[24]{0:T(128)S(1)}, f32[24]{0:T(128)}, u32[]{:S(2)}) copy-start(f32[24]{0:T(128)} %param.15) | copy-start | bytes 292
  107.3 3.2 %copy-start.1 = (f32[24,64,128]{2,1,0:T(8,128)}, f32[24,64,128]{2,1,0:T(8,128)S(1)}, u32[]{:S(2)}) copy-start(f32[24,64,128]{2,1,0:T(8,128)S(1)} %copy.59) | copy-start | bytes 2359300
Sparse Core Ops, SparseCore 0:
  75.9 24.4 reduce-scatter.3
where the time goes:
time: 118 us; the launch traced here: 117 us
  waiting for transfers between devices  30.3 us (26%)
  matrix products  24.8 us (21%)
  starting transfers between devices  14.9 us (13%)
  between operations  14.2 us (12%)
  local copies, waits for them, and re-layouts  13 us (11%)
  other arithmetic  10.4 us (9%)
  blocking collectives  9.67 us (8%)
    dot_general x2, matrix products, run_group(): jnp.einsum('ih,hgk->igk', weight_mid, hidden_one, preferred_element_type=...  15.9 us
    all_gather x1, blocking collectives, shards(): row_states = lax.all_gather(own_states, 'member', axis=0, tiled=True)  9.67 us
    ppermute x2, waiting for transfers between devices, padded_2(): lax.ppermute(lax.slice_in_dim(block, 0, width, axis=dim), axis, backward)  9.28 us
    dot_general x2, matrix products, run_group(): jnp.einsum('fj,jgk->gfk', weight_out, hidden_three, preferred_element_typ...  8.9 us
    unnamed x2, waiting for transfers between devices  8.64 us
    unnamed x18, local copies, waits for them, and re-layouts  5.76 us
    ppermute x2, waiting for transfers between devices, padded_2(): lax.ppermute(lax.slice_in_dim(block, block.shape[dim] - width, None, axis...  4.99 us
    all_to_all x1, starting transfers between devices, shards(): lax.all_to_all(outgoing, 'team', split_axis=0, concat_axis=0, tiled=True)  4.88 us
  transfers between devices with their start and end apart: 7, of which 5 were waited for; matrix products, arithmetic and copies ran while one was open for 24% of the time, Pallas kernels for 0%

commit v1 on v0

--- a/solution.py
+++ b/solution.py
@@ -82,7 +82,19 @@
     )
     picked = jnp.where(slot_valid[:, :, None, None], picked, jnp.zeros_like(picked))
     outgoing = jnp.transpose(picked, (0, 2, 1, 3)).reshape(regimes, fields, slot_width)
-    incoming = lax.all_to_all(outgoing, "team", split_axis=0, concat_axis=0, tiled=True)
+    ways, here = (lax.axis_size("team"), lax.axis_index("team"))
+    width_2 = outgoing.shape[0] // ways
+    shape = list(outgoing.shape)
+    shape[0] = width_2
+    height = shape[0]
+    shape[0] = height * ways
+    full = jnp.zeros(shape, outgoing.dtype)
+    for mask in range(ways):
+        part = lax.dynamic_slice_in_dim(outgoing, (here ^ mask) * width_2, width_2, axis=0)
+        if mask:
+            part = lax.ppermute(part, "team", [(d, d ^ mask) for d in range(ways)])
+        full = lax.dynamic_update_slice_in_dim(full, part, (here ^ mask) * height, axis=0)
+    incoming = full
     weight_in = w_in[0, 0]
     weight_mid = w_mid[0, 0]
     weight_low = w_low[0, 0]

time: 118 us -> 119 us (level)
  starting transfers between devices: 14.9 us -> 17.4 us
  waiting for transfers between devices: 30.3 us -> 28.9 us
    ppermute x0 -> x7, starting transfers between devices: none -> 8.31 us  [shards(): part = lax.ppermute(part, 'team', [(d, d ^ mask) for d in range(ways)])]
    ppermute x2, waiting for transfers between devices: 4.99 us -> 10.2 us  [padded_2(): lax.ppermute(lax.slice_in_dim(block, block.shape[dim] - width, None, axis...]
    ppermute x2, waiting for transfers between devices: 9.28 us -> 4.09 us  [padded_2(): lax.ppermute(lax.slice_in_dim(block, 0, width, axis=dim), axis, backward)]
    all_to_all x1 -> x0, starting transfers between devices: 4.88 us -> none  [shards(): lax.all_to_all(outgoing, 'team', split_axis=0, concat_axis=0, tiled=True)]
    all_to_all x1 -> x0, waiting for transfers between devices: 2.57 us -> none  [shards(): lax.all_to_all(outgoing, 'team', split_axis=0, concat_axis=0, tiled=True)]
    ppermute x2, starting transfers between devices: 2.1 us -> 0.74 us  [padded_2(): lax.ppermute(lax.slice_in_dim(block, block.shape[dim] - width, None, axis...]
    ppermute x0 -> x7, waiting for transfers between devices: none -> 1.2 us  [shards(): part = lax.ppermute(part, 'team', [(d, d ^ mask) for d in range(ways)])]
  transfers between devices with their start and end apart: 7 -> 13, of which waited for: 5 -> 5; matrix products, arithmetic and copies ran while one was open for 24% -> 24% of each run, Pallas kernels for 0% -> 0%
where the time goes in v1:
time: 119 us; the launch traced here: 118 us
  waiting for transfers between devices  28.9 us (24%)
  matrix products  24.8 us (21%)
  starting transfers between devices  17.4 us (15%)
  between operations  14.3 us (12%)
  local copies, waits for them, and re-layouts  12.5 us (11%)
  other arithmetic  10.4 us (9%)
  blocking collectives  9.67 us (8%)
    dot_general x2, matrix products, run_group(): jnp.einsum('ih,hgk->igk', weight_mid, hidden_one, preferred_element_type=...  15.9 us
    ppermute x2, waiting for transfers between devices, padded_2(): lax.ppermute(lax.slice_in_dim(block, block.shape[dim] - width, None, axis...  10.2 us
    all_gather x1, blocking collectives, shards(): row_states = lax.all_gather(own_states, 'member', axis=0, tiled=True)  9.67 us
    dot_general x2, matrix products, run_group(): jnp.einsum('fj,jgk->gfk', weight_out, hidden_three, preferred_element_typ...  8.89 us
    ppermute x7, starting transfers between devices, shards(): part = lax.ppermute(part, 'team', [(d, d ^ mask) for d in range(ways)])  8.31 us
    unnamed x2, waiting for transfers between devices  7.77 us
    unnamed x18, local copies, waits for them, and re-layouts  5.8 us
    all_to_all x1, waiting for transfers between devices, shards(): lax.all_to_all(produced, 'team', split_axis=0, concat_axis=0, tiled=True)  5.7 us
  transfers between devices with their start and end apart: 13, of which 5 were waited for; matrix products, arithmetic and copies ran while one was open for 24% of the time, Pallas kernels for 0%

profile of v1, /device:TPU:0, one launch (start us, length us, event | category | flops | bytes accessed | tf_op | source)
XLA Modules:
  0.0 118.0 jit_solution(5070818084811160119)
XLA Ops:
  7.2 0.8 fusion.50
  8.1 0.7 fusion.51
  8.8 0.7 and_bitcast_fusion
  10.2 2.8 %copy.73 = bf16[24,64,128]{0,2,1:T(8,128)(2,1)} copy(f32[24,64,128]{2,1,0:T(8,128)} %param.13) | data formatting | bytes 1179648 | tf_op args[1]
  13.0 2.5 %gather_fusion = bf16[128,24]{1,0:T(8,128)(2,1)S(1)} fusion(bf16[24,8192]{0,1:T(8,128)(2,1)} %bitcast.134, s32[1024]{0:T(1024)S(1)} %pad_clamp_fusion.1), kind=kCustom, calls=%fused_computation | custom fusion | bytes 12800 | tf_op jit(solution)/shard_map/jit(_take)/gather | solution.py:76
  15.6 9.7 %all_gather.3 = bf16[4,24,128]{2,1,0:T(8,128)(2,1)S(1)} all-gather(bf16[1,24,128]{2,1,0:T(8,128)(2,1)S(1)} %fusion.39), channel_id=1, replica_groups=mesh['team'=8,'member'=4] {'member'}, dimensions={0}, use_global_device_ids=true | all-gather | bytes 30720 | tf_op jit(solution)/shard_map/all_gather | solution.py:79
  25.3 0.6 gather_fusion.1
  26.3 1.6 %collective-permute-start.1 = (bf16[1,24,256]{2,1,0:T(8,128)(2,1)S(1)}, bf16[1,24,256]{2,1,0:T(8,128)(2,1)S(1)}, u32[]{:S(2)}, u32[]{:S(2)}) collective-permute-start(bf16[1,24,256]{2,1,0:T(8,128)(2,1)S(1)} %get-tuple-element.79), channel_id=1, source_target_pairs={{0,8},{4,12},{8,0},{12,4},{16,24},{20,28},{24,16},{28,20},{1,9},{5... | collective-permute-start | bytes 36872 | tf_op jit(solution)/shard_map/ppermute | solution.py:95
  28.0 0.2 collective-permute-start.2
  28.2 2.6 %collective-permute-start.3 = (bf16[1,24,256]{2,1,0:T(8,128)(2,1)S(1)}, bf16[1,24,256]{2,1,0:T(8,128)(2,1)S(1)}, u32[]{:S(2)}, u32[]{:S(2)}) collective-permute-start(bf16[1,24,256]{2,1,0:T(8,128)(2,1)S(1)} %get-tuple-element.77), channel_id=1, source_target_pairs={{0,16},{4,20},{8,24},{12,28},{16,0},{20,4},{24,8},{28,12},{1,17},{... | collective-permute-start | bytes 36872 | tf_op jit(solution)/shard_map/ppermute | solution.py:95
  31.0 3.6 %collective-permute-start.5 = (bf16[1,24,256]{2,1,0:T(8,128)(2,1)S(1)}, bf16[1,24,256]{2,1,0:T(8,128)(2,1)S(1)}, u32[]{:S(2)}, u32[]{:S(2)}) collective-permute-start(bf16[1,24,256]{2,1,0:T(8,128)(2,1)S(1)} %get-tuple-element.75), channel_id=1, source_target_pairs={{0,24},{4,28},{8,16},{12,20},{16,8},{20,12},{24,0},{28,4},{1,25},{... | collective-permute-start | bytes 36872 | tf_op jit(solution)/shard_map/ppermute | solution.py:95
  34.8 0.2 collective-permute-start.7
  35.0 3.3 %collective-permute-start.8 = (bf16[24,1,128]{2,1,0:T(2,128)(2,1)S(1)}, bf16[24,1,128]{2,1,0:T(2,128)(2,1)S(1)}, u32[]{:S(2)}, u32[]{:S(2)}) collective-permute-start(bf16[24,1,128]{2,1,0:T(2,128)(2,1)S(1)} %get-tuple-element.73), channel_id=1, source_target_pairs={{4,0},{8,4},{12,8},{16,12},{20,16},{24,20},{28,24},{0,28},{5,1},{9... | collective-permute-start | bytes 18440 | tf_op jit(solution)/shard_map/ppermute | solution.py:21
  38.4 1.2 %collective-permute-done.6 = bf16[1,24,256]{2,1,0:T(8,128)(2,1)S(1)} collective-permute-done((bf16[1,24,256]{2,1,0:T(8,128)(2,1)S(1)}, bf16[1,24,256]{2,1,0:T(8,128)(2,1)S(1)}, u32[]{:S(2)}, u32[]{:S(2)}) %collective-permute-start.6) | collective-permute-done | bytes 12320 | tf_op jit(solution)/shard_map/ppermute | solution.py:95
  39.6 24.8 %while.10 = (s32[]{:T(128)}, f32[2,4,24,256]{3,2,1,0:T(8,128)}, bf16[2,4,24,256]{3,2,1,0:T(8,128)(2,1)S(1)}, bf16[1600,24]{0,1:T(8,128)(2,1)S(1)}, bf16[800,1600...) while((s32[]{:T(128)}, f32[2,4,24,256]{3,2,1,0:T(8,128)}, ...), condition=%wide.region_5.6_spmd, body=%wide.region_4.5_spmd.sunk | while | flops 3389440000 | bytes 10000729 | solution.py:120
  39.6 7.9 %fusion.71 = f32[4,256,800]{1,2,0:T(8,128)} fusion(bf16[800,1600]{1,0:T(8,128)(2,1)} %get-tuple-element.149, bf16[1600,24]{0,1:T(8,128)(2,1)S(1)} %get-tuple-element.148, bf16[2,4,24,256]{3,2,1,0:T(8,128)(2,1)S(1)} %get-tuple-element.147, s32[]{:T(128)} %get-tuple-element.137), kind=kOutput, calls=%fused_computation.16.clone.1 | convolution fusion | flops 2708275200 | bytes 5965828 | tf_op jit(solution)/shard_map/while/body/eval_jaxpr/ih,hgk->igk/dot_general | solution.py:108
  47.5 4.4 %fusion.72 = f32[2,4,24,256]{3,2,1,0:T(8,128)} fusion(f32[2,4,24,256]{3,2,1,0:T(8,128)} %get-tuple-element.138, s32[]{:T(128)} %get-tuple-element.137, f32[4,256,800]{1,2,0:T(8,128)} %fusion.71, bf16[400,800]{1,0:T(8,128)(2,1)S(1)} %get-tuple-element.150, bf16[24,400]{1,0:T(8,128)(2,1)S(1)} %get-tuple-element.151), kind=kOutput, calls=%fused_computation.26.clone.1 | convolution fusion | flops 681164800 | bytes 4034816 | tf_op jit(solution)/shard_map/while/body/eval_jaxpr/fj,jgk->gfk/dot_general | solution.py:116
  52.0 7.9 %fusion.71 = f32[4,256,800]{1,2,0:T(8,128)} fusion(bf16[800,1600]{1,0:T(8,128)(2,1)} %get-tuple-element.149, bf16[1600,24]{0,1:T(8,128)(2,1)S(1)} %get-tuple-element.148, bf16[2,4,24,256]{3,2,1,0:T(8,128)(2,1)S(1)} %get-tuple-element.147, s32[]{:T(128)} %get-tuple-element.137), kind=kOutput, calls=%fused_computation.16.clone.1 | convolution fusion | flops 2708275200 | bytes 5965828 | tf_op jit(solution)/shard_map/while/body/eval_jaxpr/ih,hgk->igk/dot_general | solution.py:108
  59.9 4.5 %fusion.72 = f32[2,4,24,256]{3,2,1,0:T(8,128)} fusion(f32[2,4,24,256]{3,2,1,0:T(8,128)} %get-tuple-element.138, s32[]{:T(128)} %get-tuple-element.137, f32[4,256,800]{1,2,0:T(8,128)} %fusion.71, bf16[400,800]{1,0:T(8,128)(2,1)S(1)} %get-tuple-element.150, bf16[24,400]{1,0:T(8,128)(2,1)S(1)} %get-tuple-element.151), kind=kOutput, calls=%fused_computation.26.clone.1 | convolution fusion | flops 681164800 | bytes 4034816 | tf_op jit(solution)/shard_map/while/body/eval_jaxpr/fj,jgk->gfk/dot_general | solution.py:116
  64.4 3.4 %all-to-all-start = ((f32[8,24,256]{2,1,0:T(8,128)}), f32[8,24,256]{2,1,0:T(8,128)S(1)}, u32[]{:S(2)}, u32[]{:S(2)}) async-start(f32[8,24,256]{2,1,0:T(8,128)} %bitcast.24), calls=%async_computation | async-start | bytes 393216 | tf_op jit(solution)/shard_map/all_to_all | solution.py:121
  68.2 1.5 %collective-permute-start.10 = (bf16[24,66,1]{2,1,0:T(8,128)(2,1)S(1)}, bf16[24,66,1]{2,1,0:T(8,128)(2,1)S(1)}, u32[]{:S(2)}, u32[]{:S(2)}) collective-permute-start(bf16[24,66,1]{2,1,0:T(8,128)(2,1)S(1)} %get-tuple-element.71), channel_id=1, source_target_pairs={{1,0},{2,1},{3,2},{0,3},{5,4},{6,5},{7,6},{4,7},{9,8},{10,9},{11,1... | collective-permute-start | bytes 9512 | tf_op jit(solution)/shard_map/ppermute | solution.py:21
  69.8 0.5 collective-permute-start.9
  70.3 5.7 %all-to-all-done = f32[8,24,256]{2,1,0:T(8,128)S(1)} async-done(((f32[8,24,256]{2,1,0:T(8,128)}), f32[8,24,256]{2,1,0:T(8,128)S(1)}, u32[]{:S(2)}, u32[]{:S(2)}) %all-to-all-start) | async-done | bytes 196640 | tf_op jit(solution)/shard_map/all_to_all | solution.py:121
  76.0 1.2 gather_fusion.2
  77.2 4.1 %collective-permute-done.10 = bf16[24,66,1]{2,1,0:T(8,128)(2,1)S(1)} collective-permute-done((bf16[24,66,1]{2,1,0:T(8,128)(2,1)S(1)}, bf16[24,66,1]{2,1,0:T(8,128)(2,1)S(1)}, u32[]{:S(2)}, u32[]{:S(2)}) %collective-permute-start.10) | collective-permute-done | bytes 3200 | tf_op jit(solution)/shard_map/ppermute | solution.py:21
  81.3 10.2 %collective-permute-done.9 = bf16[24,66,1]{2,1,0:T(8,128)(2,1)} collective-permute-done((bf16[24,66,1]{2,1,0:T(8,128)(2,1)S(1)}, bf16[24,66,1]{2,1,0:T(8,128)(2,1)}, u32[]{:S(2)}, u32[]{:S(2)}) %collective-permute-start.9) | collective-permute-done | bytes 3200 | tf_op jit(solution)/shard_map/ppermute | solution.py:18
  91.5 1.7 %maximum_convert_fusion = f32[24,66,130]{2,1,0:T(8,128)S(1)} fusion(bf16[24,66,1]{2,1,0:T(8,128)(2,1)S(1)} %collective-permute-done.10, bf16[24,1,128]{2,1,0:T(2,128)(2,1)S(1)} %collective-permute-done.8, bf16[24,64,128]{2,1,0:T(8,128)(2,1)S(1)} %convert_element_type.35, bf16[24,1,128]{2,1,0:T(2,128)(2,1)S(1)} %collective-permute-done.7, ...), kind=kLoop, calls=%fused_computation.37 | loop fusion | flops 2059200 | bytes 1235520 | tf_op jit(solution)/shard_map/convert_element_type | solution.py:59
  93.2 7.8 %reduce-scatter.4.cloned.1.call-done = f32[1,24,128]{2,1,0:T(8,128)} async-done(((f32[4,24,128]{2,1,0:T(8,128)}), f32[1,24,128]{2,1,0:T(8,128)}) %reduce-scatter.4.cloned.1.call-update) | async-done | bytes 12304
  100.9 0.8 copy.78
  101.7 3.2 %scatter_custom_fusion = f32[24,8192]{0,1:T(8,128)} fusion(s32[128]{0:T(128)S(1)} %fusion.51, f32[128,24]{1,0:T(8,128)S(1)} %copy.78, f32[]{:T(128)} %constant.30.clone.1), kind=kCustom, calls=%fused_computation.35 | custom fusion | flops 3072 | bytes 786436 | tf_op jit(solution)/shard_map/scatter-add | solution.py:126
  104.9 2.9 %copy.80 = f32[24,64,128]{2,1,0:T(8,128)S(1)} copy(f32[24,64,128]{0,2,1:T(8,128)} %bitcast.133) | data formatting | bytes 1572864
  107.9 3.2 %multiply_add_fusion = f32[24,64,128]{2,1,0:T(8,128)} fusion(f32[24,64,128]{2,1,0:T(8,128)S(1)} %copy-done, f32[24,64,128]{2,1,0:T(8,128)S(1)} %copy.80, f32[24,66,130]{2,1,0:T(8,128)S(1)} %maximum_convert_fusion, f32[24,64,128]{2,1,0:T(8,128)} %param.12, f32[64,128]{1,0:T(8,128)S(1)} %get-tuple-element.83, f32[64,128]{1,0:T(8,128)S(1)} %get-tuple-element.82, ...), kind=kLoop, calls=%fused_computation.38 | loop fusion | flops 3538944 | bytes 6357088 | tf_op jit(solution)/shard_map/add | solution.py:128
  (64 shorter events, 2.1 us)
Async XLA Ops:
  7.2 23.6 %copy-start = (f32[24,64,128]{2,1,0:T(8,128)S(1)}, f32[24,64,128]{2,1,0:T(8,128)}, u32[]{:S(2)}) copy-start(f32[24,64,128]{2,1,0:T(8,128)} %param.13) | copy-start | bytes 2359300
  7.2 23.7 %copy-start.2 = (f32[2,64,128]{2,1,0:T(8,128)S(1)}, f32[2,64,128]{2,1,0:T(8,128)}, u32[]{:S(2)}) copy-start(f32[2,64,128]{2,1,0:T(8,128)} %param.14) | copy-start | bytes 196612
  9.9 21.0 %copy-start.4 = (s32[32,1]{0,1:T(1,128)S(1)}, s32[32,1]{0,1:T(1,128)}, u32[]{:S(2)}) copy-start(s32[32,1]{0,1:T(1,128)} %param.17) | copy-start | bytes 388
  10.2 29.4 %copy-start.5 = (bf16[1,1,400,800]{3,2,1,0:T(8,128)(2,1)S(1)}, bf16[1,1,400,800]{3,2,1,0:T(8,128)(2,1)}, u32[]{:S(2)}) copy-start(bf16[1,1,400,800]{3,2,1,0:T(8,128)(2,1)} %param.20) | copy-start | bytes 1920004
  10.2 29.4 %copy-start.6 = (bf16[1,1,1600,24]{2,3,1,0:T(8,128)(2,1)S(1)}, bf16[1,1,1600,24]{2,3,1,0:T(8,128)(2,1)}, u32[]{:S(2)}) copy-start(bf16[1,1,1600,24]{2,3,1,0:T(8,128)(2,1)} %param.18) | copy-start | bytes 230404
  10.2 29.4 %copy-start.7 = (bf16[1,1,24,400]{3,2,1,0:T(8,128)(2,1)S(1)}, bf16[1,1,24,400]{3,2,1,0:T(8,128)(2,1)}, u32[]{:S(2)}) copy-start(bf16[1,1,24,400]{3,2,1,0:T(8,128)(2,1)} %param.21) | copy-start | bytes 57604
  26.2 4.8 %collective-permute-start = (bf16[1,24,256]{2,1,0:T(8,128)(2,1)S(1)}, bf16[1,24,256]{2,1,0:T(8,128)(2,1)S(1)}, u32[]{:S(2)}, u32[]{:S(2)}) collective-permute-start(bf16[1,24,256]{2,1,0:T(8,128)(2,1)S(1)} %get-tuple-element.80), channel_id=1, source_target_pairs={{0,4},{4,0},{8,12},{12,8},{16,20},{20,16},{24,28},{28,24},{1,5},{5... | collective-permute-start | bytes 36872 | tf_op jit(solution)/shard_map/ppermute | solution.py:95
  26.3 8.3 %collective-permute-start.1 = (bf16[1,24,256]{2,1,0:T(8,128)(2,1)S(1)}, bf16[1,24,256]{2,1,0:T(8,128)(2,1)S(1)}, u32[]{:S(2)}, u32[]{:S(2)}) collective-permute-start(bf16[1,24,256]{2,1,0:T(8,128)(2,1)S(1)} %get-tuple-element.79), channel_id=1, source_target_pairs={{0,8},{4,12},{8,0},{12,4},{16,24},{20,28},{24,16},{28,20},{1,9},{5... | collective-permute-start | bytes 36872 | tf_op jit(solution)/shard_map/ppermute | solution.py:95
  28.0 6.8 %collective-permute-start.2 = (bf16[1,24,256]{2,1,0:T(8,128)(2,1)S(1)}, bf16[1,24,256]{2,1,0:T(8,128)(2,1)S(1)}, u32[]{:S(2)}, u32[]{:S(2)}) collective-permute-start(bf16[1,24,256]{2,1,0:T(8,128)(2,1)S(1)} %get-tuple-element.78), channel_id=1, source_target_pairs={{0,12},{4,8},{8,4},{12,0},{16,28},{20,24},{24,20},{28,16},{1,13},{... | collective-permute-start | bytes 36872 | tf_op jit(solution)/shard_map/ppermute | solution.py:95
  28.2 6.8 %collective-permute-start.3 = (bf16[1,24,256]{2,1,0:T(8,128)(2,1)S(1)}, bf16[1,24,256]{2,1,0:T(8,128)(2,1)S(1)}, u32[]{:S(2)}, u32[]{:S(2)}) collective-permute-start(bf16[1,24,256]{2,1,0:T(8,128)(2,1)S(1)} %get-tuple-element.77), channel_id=1, source_target_pairs={{0,16},{4,20},{8,24},{12,28},{16,0},{20,4},{24,8},{28,12},{1,17},{... | collective-permute-start | bytes 36872 | tf_op jit(solution)/shard_map/ppermute | solution.py:95
  30.8 7.6 %collective-permute-start.4 = (bf16[1,24,256]{2,1,0:T(8,128)(2,1)S(1)}, bf16[1,24,256]{2,1,0:T(8,128)(2,1)S(1)}, u32[]{:S(2)}, u32[]{:S(2)}) collective-permute-start(bf16[1,24,256]{2,1,0:T(8,128)(2,1)S(1)} %get-tuple-element.76), channel_id=1, source_target_pairs={{0,20},{4,16},{8,28},{12,24},{16,4},{20,0},{24,12},{28,8},{1,21},{... | collective-permute-start | bytes 36872 | tf_op jit(solution)/shard_map/ppermute | solution.py:95
  31.0 7.4 %collective-permute-start.5 = (bf16[1,24,256]{2,1,0:T(8,128)(2,1)S(1)}, bf16[1,24,256]{2,1,0:T(8,128)(2,1)S(1)}, u32[]{:S(2)}, u32[]{:S(2)}) collective-permute-start(bf16[1,24,256]{2,1,0:T(8,128)(2,1)S(1)} %get-tuple-element.75), channel_id=1, source_target_pairs={{0,24},{4,28},{8,16},{12,20},{16,8},{20,12},{24,0},{28,4},{1,25},{... | collective-permute-start | bytes 36872 | tf_op jit(solution)/shard_map/ppermute | solution.py:95
  34.7 4.9 %collective-permute-start.6 = (bf16[1,24,256]{2,1,0:T(8,128)(2,1)S(1)}, bf16[1,24,256]{2,1,0:T(8,128)(2,1)S(1)}, u32[]{:S(2)}, u32[]{:S(2)}) collective-permute-start(bf16[1,24,256]{2,1,0:T(8,128)(2,1)S(1)} %get-tuple-element.74), channel_id=1, source_target_pairs={{0,28},{4,24},{8,20},{12,16},{16,12},{20,8},{24,4},{28,0},{1,29},{... | collective-permute-start | bytes 36872 | tf_op jit(solution)/shard_map/ppermute | solution.py:95
  34.8 33.0 %collective-permute-start.7 = (bf16[24,1,128]{2,1,0:T(2,128)(2,1)S(1)}, bf16[24,1,128]{2,1,0:T(2,128)(2,1)S(1)}, u32[]{:S(2)}, u32[]{:S(2)}) collective-permute-start(bf16[24,1,128]{2,1,0:T(2,128)(2,1)S(1)} %get-tuple-element.72), channel_id=1, source_target_pairs={{0,4},{4,8},{8,12},{12,16},{16,20},{20,24},{24,28},{28,0},{1,5},{5... | collective-permute-start | bytes 18440 | tf_op jit(solution)/shard_map/ppermute | solution.py:18
  35.0 32.8 %collective-permute-start.8 = (bf16[24,1,128]{2,1,0:T(2,128)(2,1)S(1)}, bf16[24,1,128]{2,1,0:T(2,128)(2,1)S(1)}, u32[]{:S(2)}, u32[]{:S(2)}) collective-permute-start(bf16[24,1,128]{2,1,0:T(2,128)(2,1)S(1)} %get-tuple-element.73), channel_id=1, source_target_pairs={{4,0},{8,4},{12,8},{16,12},{20,16},{24,20},{28,24},{0,28},{5,1},{9... | collective-permute-start | bytes 18440 | tf_op jit(solution)/shard_map/ppermute | solution.py:21
  64.4 11.6 %all-to-all-start = ((f32[8,24,256]{2,1,0:T(8,128)}), f32[8,24,256]{2,1,0:T(8,128)S(1)}, u32[]{:S(2)}, u32[]{:S(2)}) async-start(f32[8,24,256]{2,1,0:T(8,128)} %bitcast.24), calls=%async_computation | async-start | bytes 393216 | tf_op jit(solution)/shard_map/all_to_all | solution.py:121
  67.8 33.2 %reduce-scatter.4.cloned.1.call-start = ((), (), s32[]{:S(2)}) async-start(), calls=%async_computation.2 | async-start | bytes 61440
  68.2 13.1 %collective-permute-start.10 = (bf16[24,66,1]{2,1,0:T(8,128)(2,1)S(1)}, bf16[24,66,1]{2,1,0:T(8,128)(2,1)S(1)}, u32[]{:S(2)}, u32[]{:S(2)}) collective-permute-start(bf16[24,66,1]{2,1,0:T(8,128)(2,1)S(1)} %get-tuple-element.71), channel_id=1, source_target_pairs={{1,0},{2,1},{3,2},{0,3},{5,4},{6,5},{7,6},{4,7},{9,8},{10,9},{11,1... | collective-permute-start | bytes 9512 | tf_op jit(solution)/shard_map/ppermute | solution.py:21
  69.8 21.7 %collective-permute-start.9 = (bf16[24,66,1]{2,1,0:T(8,128)(2,1)S(1)}, bf16[24,66,1]{2,1,0:T(8,128)(2,1)}, u32[]{:S(2)}, u32[]{:S(2)}) collective-permute-start(bf16[24,66,1]{2,1,0:T(8,128)(2,1)S(1)} %get-tuple-element.70), channel_id=1, source_target_pairs={{0,1},{1,2},{2,3},{3,0},{4,5},{5,6},{6,7},{7,4},{8,9},{9,10},{10,1... | collective-permute-start | bytes 9512 | tf_op jit(solution)/shard_map/ppermute | solution.py:18
  104.9 3.0 %copy-start.3 = (f32[24]{0:T(128)S(1)}, f32[24]{0:T(128)}, u32[]{:S(2)}) copy-start(f32[24]{0:T(128)} %param.15) | copy-start | bytes 292
  107.9 3.2 %copy-start.1 = (f32[24,64,128]{2,1,0:T(8,128)}, f32[24,64,128]{2,1,0:T(8,128)S(1)}, u32[]{:S(2)}) copy-start(f32[24,64,128]{2,1,0:T(8,128)S(1)} %copy.80) | copy-start | bytes 2359300
Sparse Core Ops, SparseCore 0:
  77.3 23.5 reduce-scatter.3
